TPU v7x, 32 devices: a whole 2x2x4 slice. The times are simulated.
32 devices in a mesh: sub: 8 (over y, x, core), coarse: 4 (over z).
Axes of the slice: x: 2, y: 2, z: 4, core: 2. Of those that a mesh axis runs over, the one named last changes fastest.
Arguments:
- right_side: float32 [8, 4, 128, 128], P('sub', 'coarse'), may hold values from -150 to 150
- diagonal: float32 [8, 4, 128, 128], P('sub', 'coarse'), may hold values from 2 to 8
- cell_link: float32 [8, 4, 128, 128], P('sub', 'coarse'), may hold values from 0.2 to 0.9
- block_inverse: float32 [8, 4, 128, 128, 128], P('sub', 'coarse'), may hold values from -1 to 1
- coupling: float32 [8, 4, 4, 128, 128], P('sub', 'coarse'), may hold values from -0.26516503 to 0.26516503
- coarse_basis: float32 [8, 4, 128, 128], P('sub', 'coarse'), may hold values from -6 to 6
- coarse_inverse: float32 [512, 512], P('coarse'), may hold values from -0.25 to 0.25
- partner: int32 [8, 4], P('sub'), may hold values from 0 to 7, as said below
- margin_width: int32 [8, 4], P('sub'), may hold values from 4 to 8, as said below
- margin_blocks: int32 [8, 4, 4, 8], P('sub', 'coarse'), may hold values from 0 to 127
- aggregate: int32 [8, 4, 128], P('sub', 'coarse'), may hold values from 0 to 511, as said below
Outputs:
- solution: float32 [8, 4, 128, 128], P('sub', 'coarse')
Inputs may be any that keep to these rules, and one draw needn't show every extreme that they name: partner[s, r] differs from s, partner[partner[s, r], r] = s, and the 4 partners of one subdomain are distinct. margin_width[partner[s, r], r] = margin_width[s, r]; every colour round has a pair with width 8. `margin_blocks`: entries with w >= margin_width[s, r] are not used. aggregate[s, c, b] lies in (s * 4 + c) * 16 to (s * 4 + c + 1) * 16 - 1, and every one of these 16 aggregates has a block of part [s, c].
All inputs are finite; a program needn't handle non-finite values.
Results may differ from a plain program's by a relative error of at most 0.0003.
Values sent between devices are 32-bit elements; how exact they have to be, the bound alone decides.
No kernel may reach another device: no remote copies, remote signals or barrier semaphores. Data moves between devices by JAX's collectives and lax.ppermute only.
A program may use at most 64 MiB of HBM per device.

v0:
```python
import jax
import jax.numpy as jnp
from jax import lax
from jax.sharding import PartitionSpec as P

BS = 128
BPD = 128
AGG_DEV = 16
ITERS = 4


def givens_solve(columns, beta):
    steps_count = len(columns)
    cosines = []
    sines = []
    side_terms = [beta] + [jnp.zeros_like(beta) for unused in range(steps_count)]
    triangle = []
    for column_id in range(steps_count):
        column = list(columns[column_id])
        for row_id in range(column_id):
            upper = column[row_id]
            lower = column[row_id + 1]
            column[row_id] = cosines[row_id] * upper + sines[row_id] * lower
            column[row_id + 1] = cosines[row_id] * lower - sines[row_id] * upper
        upper = column[column_id]
        lower = column[column_id + 1]
        radius = jnp.sqrt(upper * upper + lower * lower)
        cosine = upper / radius
        sine_value = lower / radius
        column[column_id] = radius
        cosines.append(cosine)
        sines.append(sine_value)
        side_terms[column_id + 1] = -sine_value * side_terms[column_id]
        side_terms[column_id] = cosine * side_terms[column_id]
        triangle.append(column)
    weights = [None] * steps_count
    for column_id in reversed(range(steps_count)):
        running = side_terms[column_id]
        for later_col in range(column_id + 1, steps_count):
            running = running - triangle[later_col][column_id] * weights[later_col]
        weights[column_id] = running / triangle[column_id][column_id]
    return weights


def on_device(
    right_side,
    diagonal,
    cell_link,
    block_inverse,
    coupling,
    coarse_basis,
    coarse_inverse,
    partner,
    margin_width,
    margin_blocks,
    aggregate,
):
    highest = lax.Precision.HIGHEST
    block_count = right_side.shape[2]
    unknowns = right_side.shape[3]
    factor = (BS * BPD / AGG_DEV) ** (-0.5)
    inverse_blocks = block_inverse[0, 0]
    couplings = coupling[0, 0]
    basis_local = coarse_basis[0, 0]
    diagonal_local = diagonal[0, 0]
    link_local = cell_link[0, 0]
    paired = partner[0]
    widths = margin_width[0]
    blocks = margin_blocks[0, 0]
    member_of = aggregate[0, 0]
    aggregate_count = coarse_inverse.shape[1]
    member_table = (member_of[:, None] == jnp.arange(aggregate_count)[None, :]).astype(jnp.float32)
    rounds = blocks.shape[0]
    widest = blocks.shape[1]
    target = (blocks.reshape(-1)[:, None] == jnp.arange(block_count)[None, :]).astype(jnp.float32)
    live_mask = (jnp.arange(widest)[None, :] < widths[:, None]).astype(jnp.float32)

    def margin(values):
        outgoing = jnp.take(values, blocks.reshape(-1), axis=0).reshape(rounds, widest, unknowns)
        pieces = []
        for round_id in range(rounds):
            gathered = lax.all_gather(outgoing[round_id], "sub", axis=0, tiled=True)
            pieces.append(lax.dynamic_slice_in_dim(gathered, paired[round_id] * widest, widest, 0))
        incoming = jnp.stack(pieces)
        mapped = (
            jnp.einsum("rij,rwj->rwi", couplings, incoming, precision=highest)
            * live_mask[:, :, None]
        )
        return jnp.einsum(
            "kb,ki->bi", target, mapped.reshape(rounds * widest, unknowns), precision=highest
        )

    def squared_norm(values):
        return lax.psum(jnp.sum(values * values), ("sub", "coarse"))

    start_vector = right_side[0, 0]
    directions = []
    columns = []
    beta = jnp.sqrt(squared_norm(start_vector))
    basis_list = [start_vector / beta]
    for krylov_step in range(ITERS):
        current = basis_list[-1]
        inner = jnp.sum(basis_local * current, axis=1)
        restricted = lax.psum(
            jnp.dot(inner, member_table, precision=highest) * factor, ("sub", "coarse")
        )
        local_part = jnp.einsum(
            "bij,bj->bi", inverse_blocks, current + margin(current), precision=highest
        )
        coarse_part = jnp.dot(coarse_inverse, restricted, precision=highest)
        coarse_full = lax.all_gather(coarse_part, "coarse", axis=0, tiled=True)
        prolonged = jnp.dot(member_table, coarse_full, precision=highest)
        direction = local_part + prolonged[:, None] * basis_local
        directions.append(direction)
        flat_line = direction.reshape(-1)
        link_line = link_local.reshape(-1)
        zero_pad = jnp.zeros((1,), jnp.float32)
        ahead_terms = jnp.concatenate([flat_line[1:], zero_pad]) * link_line
        behind_terms = jnp.concatenate([zero_pad, (link_line * flat_line)[:-1]])
        product = (
            diagonal_local * direction
            - (ahead_terms + behind_terms).reshape(direction.shape)
            - margin(direction)
        )
        projected = lax.psum(
            jnp.stack([jnp.sum(vector * product) for vector in basis_list]), ("sub", "coarse")
        )
        for position in range(len(basis_list)):
            product = product - projected[position] * basis_list[position]
        norm_new = jnp.sqrt(squared_norm(product))
        columns.append([projected[position] for position in range(len(basis_list))] + [norm_new])
        basis_list.append(product / norm_new)
    weights = givens_solve(columns, beta)
    solution = weights[0] * directions[0]
    for position in range(1, ITERS):
        solution = solution + weights[position] * directions[position]
    return solution.reshape(right_side.shape)


def solution(mesh):
    placed = (
        P("sub", "coarse", None, None),
        P("sub", "coarse", None, None),
        P("sub", "coarse", None, None),
        P("sub", "coarse", None, None, None),
        P("sub", "coarse", None, None, None),
        P("sub", "coarse", None, None),
        P("coarse", None),
        P("sub", None),
        P("sub", None),
        P("sub", "coarse", None, None),
        P("sub", "coarse", None),
    )
    return jax.shard_map(
        on_device,
        mesh=mesh,
        in_specs=placed,
        out_specs=P("sub", "coarse", None, None),
        check_vma=False,
    )
```

profile of v0, /device:TPU:0, one launch (start us, length us, event | category | flops | bytes accessed | tf_op | source)
XLA Modules:
  0.0 958.9 jit_solution(15861982066872133460)
XLA Ops:
  0.9 1.5 multiply_reduce_fusion.14
  2.3 42.2 %psum.91 = f32[]{:T(128)} all-reduce(f32[]{:T(128)} %multiply_reduce_fusion.14), channel_id=1, replica_groups=mesh['sub'=8,'coarse'=4] {'sub','coarse'}, use_global_device_ids=true, to_apply=%region_1.0 | all-reduce | flops 1 | bytes 8 | tf_op jit(solution)/shard_map/psum | solution.py:94
  46.9 10.0 %all_gather.108 = f32[64,128]{1,0:T(8,128)S(1)} all-gather(f32[8,128]{1,0:T(8,128)S(1)} %get-tuple-element.63), channel_id=1, replica_groups=mesh['sub'=8,'coarse'=4] {'sub'}, dimensions={0}, use_global_device_ids=true | all-gather | bytes 36864 | tf_op jit(solution)/shard_map/all_gather | solution.py:82
  56.9 1.5 fusion.188
  59.0 8.1 all_gather.109
  67.9 9.1 all_gather.110
  77.6 8.1 all_gather.111
  87.8 15.4 %fusion.6 = f32[128,1,128]{2,1,0:T(1,128)S(1)} fusion(f32[128,128,1]{1,2,0:T(1,128)S(1)} %bitcast.355, f32[1,1,128,128,128]{4,3,2,1,0:T(8,128)} %param.16), kind=kOutput, calls=%fused_computation.14 | convolution fusion | flops 25165824 | bytes 8519680 | tf_op jit(solution)/shard_map/bij,bj->bi/dot_general | solution.py:107
  103.5 39.4 %psum.92 = f32[512]{0:T(512)S(1)} all-reduce(f32[512]{0:T(512)S(1)} %broadcast_multiply_fusion.3), channel_id=1, replica_groups=mesh['sub'=8,'coarse'=4] {'sub','coarse'}, use_global_device_ids=true, to_apply=%region_3.5 | all-reduce | flops 512 | bytes 4096 | tf_op jit(solution)/shard_map/psum | solution.py:104
  143.1 9.8 %all-gather = f32[4,1,128]{2,1,0:T(1,128)S(1)} all-gather(f32[1,1,128]{2,1,0:T(1,128)S(1)} %convolution_bitcast_fusion.7), channel_id=1, replica_groups=mesh['sub'=8,'coarse'=4] {'coarse'}, dimensions={0}, use_global_device_ids=true | all-gather | bytes 2560 | tf_op jit(solution)/shard_map/all_gather | solution.py:111
  153.9 9.8 %all_gather.113 = f32[64,128]{1,0:T(8,128)S(1)} all-gather(f32[8,128]{1,0:T(8,128)S(1)} %get-tuple-element.59), channel_id=1, replica_groups=mesh['sub'=8,'coarse'=4] {'sub'}, dimensions={0}, use_global_device_ids=true | all-gather | bytes 36864 | tf_op jit(solution)/shard_map/all_gather | solution.py:82
  163.8 9.1 all_gather.114
  172.8 8.1 all_gather.115
  180.9 9.1 all_gather.116
  191.5 37.8 %psum.93 = f32[]{:T(128)} all-reduce(f32[]{:T(128)} %get-tuple-element.80), channel_id=1, replica_groups=mesh['sub'=8,'coarse'=4] {'sub','coarse'}, use_global_device_ids=true, to_apply=%region_5.7 | all-reduce | flops 1 | bytes 8 | tf_op jit(solution)/shard_map/psum | solution.py:125
  229.3 1.3 multiply_reduce_fusion.12
  230.6 41.2 %psum.94 = f32[]{:T(128)} all-reduce(f32[]{:T(128)} %multiply_reduce_fusion.12), channel_id=1, replica_groups=mesh['sub'=8,'coarse'=4] {'sub','coarse'}, use_global_device_ids=true, to_apply=%region_7.9 | all-reduce | flops 1 | bytes 8 | tf_op jit(solution)/shard_map/psum | solution.py:94
  274.0 10.1 %all_gather.117 = f32[64,128]{1,0:T(8,128)S(1)} all-gather(f32[8,128]{1,0:T(8,128)S(1)} %get-tuple-element.55), channel_id=1, replica_groups=mesh['sub'=8,'coarse'=4] {'sub'}, dimensions={0}, use_global_device_ids=true | all-gather | bytes 36864 | tf_op jit(solution)/shard_map/all_gather | solution.py:82
  284.1 9.0 all_gather.118
  293.1 8.1 all_gather.119
  301.2 9.0 all_gather.120
  311.1 15.4 %fusion.4 = f32[128,1,128]{2,1,0:T(1,128)S(1)} fusion(f32[128,128,1]{1,2,0:T(1,128)S(1)} %bitcast.356, f32[1,1,128,128,128]{4,3,2,1,0:T(8,128)} %param.16), kind=kOutput, calls=%fused_computation.12 | convolution fusion | flops 25165824 | bytes 8519680 | tf_op jit(solution)/shard_map/bij,bj->bi/dot_general | solution.py:107
  326.8 37.7 %psum.95 = f32[512]{0:T(512)S(1)} all-reduce(f32[512]{0:T(512)S(1)} %broadcast_multiply_fusion.2), channel_id=1, replica_groups=mesh['sub'=8,'coarse'=4] {'sub','coarse'}, use_global_device_ids=true, to_apply=%region_9.11 | all-reduce | flops 512 | bytes 4096 | tf_op jit(solution)/shard_map/psum | solution.py:104
  364.7 9.6 %all-gather.1 = f32[4,1,128]{2,1,0:T(1,128)S(1)} all-gather(f32[1,1,128]{2,1,0:T(1,128)S(1)} %convolution_bitcast_fusion.5), channel_id=1, replica_groups=mesh['sub'=8,'coarse'=4] {'coarse'}, dimensions={0}, use_global_device_ids=true | all-gather | bytes 2560 | tf_op jit(solution)/shard_map/all_gather | solution.py:111
  375.4 9.8 %all_gather.122 = f32[64,128]{1,0:T(8,128)S(1)} all-gather(f32[8,128]{1,0:T(8,128)S(1)} %get-tuple-element.51), channel_id=1, replica_groups=mesh['sub'=8,'coarse'=4] {'sub'}, dimensions={0}, use_global_device_ids=true | all-gather | bytes 36864 | tf_op jit(solution)/shard_map/all_gather | solution.py:82
  385.2 8.1 all_gather.123
  393.3 9.0 all_gather.124
  402.3 8.3 all_gather.125
  411.2 1.0 multiply_reduce_fusion.11
  412.2 1.3 pad_maximum_fusion.8
  413.5 37.6 %psum.96 = f32[2]{0:T(128)S(1)} all-reduce(f32[2]{0:T(128)S(1)} %pad_maximum_fusion.8), channel_id=1, replica_groups=mesh['sub'=8,'coarse'=4] {'sub','coarse'}, use_global_device_ids=true, to_apply=%region_12.14 | all-reduce | flops 2 | bytes 16 | tf_op jit(solution)/shard_map/psum | solution.py:125
  451.8 1.9 multiply_reduce_fusion.9
  453.6 41.7 %psum.97 = f32[]{:T(128)} all-reduce(f32[]{:T(128)} %get-tuple-element.21), channel_id=1, replica_groups=mesh['sub'=8,'coarse'=4] {'sub','coarse'}, use_global_device_ids=true, to_apply=%region_14.16 | all-reduce | flops 1 | bytes 8 | tf_op jit(solution)/shard_map/psum | solution.py:94
  496.8 10.1 %all_gather.126 = f32[64,128]{1,0:T(8,128)S(1)} all-gather(f32[8,128]{1,0:T(8,128)S(1)} %get-tuple-element.47), channel_id=1, replica_groups=mesh['sub'=8,'coarse'=4] {'sub'}, dimensions={0}, use_global_device_ids=true | all-gather | bytes 36864 | tf_op jit(solution)/shard_map/all_gather | solution.py:82
  506.9 8.1 all_gather.127
  515.0 9.0 all_gather.128
  524.0 8.1 all_gather.129
  533.0 15.4 %fusion.2 = f32[128,1,128]{2,1,0:T(1,128)S(1)} fusion(f32[128,128,1]{1,2,0:T(1,128)S(1)} %bitcast.357, f32[1,1,128,128,128]{4,3,2,1,0:T(8,128)} %param.16), kind=kOutput, calls=%fused_computation.10 | convolution fusion | flops 25165824 | bytes 8519680 | tf_op jit(solution)/shard_map/bij,bj->bi/dot_general | solution.py:107
  548.6 37.7 %psum.98 = f32[512]{0:T(512)S(1)} all-reduce(f32[512]{0:T(512)S(1)} %broadcast_multiply_fusion.1), channel_id=1, replica_groups=mesh['sub'=8,'coarse'=4] {'sub','coarse'}, use_global_device_ids=true, to_apply=%region_16.18 | all-reduce | flops 512 | bytes 4096 | tf_op jit(solution)/shard_map/psum | solution.py:104
  586.5 9.6 %all-gather.2 = f32[4,1,128]{2,1,0:T(1,128)S(1)} all-gather(f32[1,1,128]{2,1,0:T(1,128)S(1)} %convolution_bitcast_fusion.3), channel_id=1, replica_groups=mesh['sub'=8,'coarse'=4] {'coarse'}, dimensions={0}, use_global_device_ids=true | all-gather | bytes 2560 | tf_op jit(solution)/shard_map/all_gather | solution.py:111
  597.2 9.8 %all_gather.131 = f32[64,128]{1,0:T(8,128)S(1)} all-gather(f32[8,128]{1,0:T(8,128)S(1)} %get-tuple-element.43), channel_id=1, replica_groups=mesh['sub'=8,'coarse'=4] {'sub'}, dimensions={0}, use_global_device_ids=true | all-gather | bytes 36864 | tf_op jit(solution)/shard_map/all_gather | solution.py:82
  607.0 9.0 all_gather.132
  616.1 8.5 all_gather.133
  624.6 9.0 all_gather.134
  635.2 1.9 pad_maximum_fusion.9
  637.2 37.6 %psum.99 = f32[3]{0:T(128)S(1)} all-reduce(f32[3]{0:T(128)S(1)} %pad_maximum_fusion.9), channel_id=1, replica_groups=mesh['sub'=8,'coarse'=4] {'sub','coarse'}, use_global_device_ids=true, to_apply=%region_20.22 | all-reduce | flops 3 | bytes 24 | tf_op jit(solution)/shard_map/psum | solution.py:125
  675.4 2.5 multiply_reduce_fusion.5
  677.9 40.7 %psum.100 = f32[]{:T(128)} all-reduce(f32[]{:T(128)} %get-tuple-element.17), channel_id=1, replica_groups=mesh['sub'=8,'coarse'=4] {'sub','coarse'}, use_global_device_ids=true, to_apply=%region_22.24 | all-reduce | flops 1 | bytes 8 | tf_op jit(solution)/shard_map/psum | solution.py:94
  720.0 10.0 %all_gather.135 = f32[64,128]{1,0:T(8,128)S(1)} all-gather(f32[8,128]{1,0:T(8,128)S(1)} %get-tuple-element.39), channel_id=1, replica_groups=mesh['sub'=8,'coarse'=4] {'sub'}, dimensions={0}, use_global_device_ids=true | all-gather | bytes 36864 | tf_op jit(solution)/shard_map/all_gather | solution.py:82
  730.0 9.0 all_gather.136
  739.1 8.1 all_gather.137
  747.1 9.0 all_gather.138
  757.1 15.4 %fusion = f32[128,1,128]{2,1,0:T(1,128)S(1)} fusion(f32[128,128,1]{1,2,0:T(1,128)S(1)} %bitcast.358, f32[1,1,128,128,128]{4,3,2,1,0:T(8,128)} %param.16), kind=kOutput, calls=%fused_computation.8 | convolution fusion | flops 25165824 | bytes 8519680 | tf_op jit(solution)/shard_map/bij,bj->bi/dot_general | solution.py:107
  772.7 37.7 %psum.101 = f32[512]{0:T(512)S(1)} all-reduce(f32[512]{0:T(512)S(1)} %broadcast_multiply_fusion), channel_id=1, replica_groups=mesh['sub'=8,'coarse'=4] {'sub','coarse'}, use_global_device_ids=true, to_apply=%region_24.26 | all-reduce | flops 512 | bytes 4096 | tf_op jit(solution)/shard_map/psum | solution.py:104
  810.6 9.6 %all-gather.3 = f32[4,1,128]{2,1,0:T(1,128)S(1)} all-gather(f32[1,1,128]{2,1,0:T(1,128)S(1)} %convolution_bitcast_fusion.1), channel_id=1, replica_groups=mesh['sub'=8,'coarse'=4] {'coarse'}, dimensions={0}, use_global_device_ids=true | all-gather | bytes 2560 | tf_op jit(solution)/shard_map/all_gather | solution.py:111
  821.3 9.8 %all_gather.140 = f32[64,128]{1,0:T(8,128)S(1)} all-gather(f32[8,128]{1,0:T(8,128)S(1)} %get-tuple-element.35), channel_id=1, replica_groups=mesh['sub'=8,'coarse'=4] {'sub'}, dimensions={0}, use_global_device_ids=true | all-gather | bytes 36864 | tf_op jit(solution)/shard_map/all_gather | solution.py:82
  831.1 8.2 all_gather.141
  839.4 9.0 all_gather.142
  848.4 8.1 all_gather.143
  857.1 1.0 multiply_reduce_fusion.4
  858.1 2.5 pad_maximum_fusion.10
  860.6 37.6 %psum.102 = f32[4]{0:T(128)S(1)} all-reduce(f32[4]{0:T(128)S(1)} %pad_maximum_fusion.10), channel_id=1, replica_groups=mesh['sub'=8,'coarse'=4] {'sub','coarse'}, use_global_device_ids=true, to_apply=%region_29.31 | all-reduce | flops 4 | bytes 32 | tf_op jit(solution)/shard_map/psum | solution.py:125
  905.5 3.0 multiply_reduce_fusion
  908.5 41.8 %psum.103 = f32[]{:T(128)} all-reduce(f32[]{:T(128)} %multiply_reduce_fusion), channel_id=1, replica_groups=mesh['sub'=8,'coarse'=4] {'sub','coarse'}, use_global_device_ids=true, to_apply=%region_31.33 | all-reduce | flops 1 | bytes 8 | tf_op jit(solution)/shard_map/psum | solution.py:94
  (119 shorter events, 22.8 us)
Async XLA Ops:
  0.0 87.0 %copy-start = (f32[1,1,4,128,128]{4,3,2,1,0:T(8,128)S(1)}, f32[1,1,4,128,128]{4,3,2,1,0:T(8,128)}, u32[]{:S(2)}) copy-start(f32[1,1,4,128,128]{4,3,2,1,0:T(8,128)} %param.17) | copy-start | bytes 786436
  0.0 153.1 %copy-start.1 = (f32[1,1,128,128]{3,2,1,0:T(8,128)S(1)}, f32[1,1,128,128]{3,2,1,0:T(8,128)}, u32[]{:S(2)}) copy-start(f32[1,1,128,128]{3,2,1,0:T(8,128)} %param.18) | copy-start | bytes 196612
  0.0 103.2 %copy-start.5 = (s32[1,1,128]{2,1,0:T(1,128)S(1)}, s32[1,1,128]{2,1,0:T(1,128)}, u32[]{:S(2)}) copy-start(s32[1,1,128]{2,1,0:T(1,128)} %param.23) | copy-start | bytes 1540
  0.0 142.9 %copy-start.2 = (f32[128,512]{1,0:T(8,128)S(1)}, f32[128,512]{1,0:T(8,128)}, u32[]{:S(2)}) copy-start(f32[128,512]{1,0:T(8,128)} %param.19) | copy-start | bytes 786436
  0.0 190.4 %copy-start.3 = (f32[1,1,128,128]{3,2,1,0:T(8,128)S(1)}, f32[1,1,128,128]{3,2,1,0:T(8,128)}, u32[]{:S(2)}) copy-start(f32[1,1,128,128]{3,2,1,0:T(8,128)} %param.15) | copy-start | bytes 196612
  0.0 190.5 %copy-start.4 = (f32[1,1,128,128]{3,2,1,0:T(8,128)S(1)}, f32[1,1,128,128]{3,2,1,0:T(8,128)}, u32[]{:S(2)}) copy-start(f32[1,1,128,128]{3,2,1,0:T(8,128)} %param.14) | copy-start | bytes 196612
where the time goes:
time: 971 us; the launch traced here: 959 us
  blocking collectives  835 us (86%)
  matrix products  73.9 us (8%)
  other arithmetic  21.1 us (2%)
  between operations  20.1 us (2%)
    all_gather x32, blocking collectives, margin(): gathered = lax.all_gather(outgoing[round_id], 'sub', axis=0, tiled=True)  286 us
    psum x5, blocking collectives, squared_norm(): return lax.psum(jnp.sum(values * values), ('sub', 'coarse'))  208 us
    psum x4, blocking collectives, on_device(): lax.psum(jnp.dot(inner, member_table, precision=highest) * factor, ('sub'...  152 us
    psum x4, blocking collectives, on_device(): lax.psum(jnp.stack([jnp.sum(vector * product) for vector in basis_list]),...  151 us
    dot_general x4, matrix products, on_device(): jnp.einsum('bij,bj->bi', inverse_blocks, current + margin(current), preci...  61.5 us
    all_gather x4, blocking collectives, on_device(): coarse_full = lax.all_gather(coarse_part, 'coarse', axis=0, tiled=True)  38.7 us

commit v1 on v0

--- a/solution.py
+++ b/solution.py
@@ -108,7 +108,22 @@
             "bij,bj->bi", inverse_blocks, current + margin(current), precision=highest
         )
         coarse_part = jnp.dot(coarse_inverse, restricted, precision=highest)
-        coarse_full = lax.all_gather(coarse_part, "coarse", axis=0, tiled=True)
+        size, index, rows = (
+            lax.axis_size("coarse"),
+            lax.axis_index("coarse"),
+            coarse_part.shape[0],
+        )
+        right = [(i, (i + 1) % size) for i in range(size)]
+        out = jnp.zeros(
+            (*coarse_part.shape[:0], size * rows, *coarse_part.shape[0 + 1 :]), coarse_part.dtype
+        )
+        held = coarse_part
+        for hop in range(size):
+            owner = (index - hop) % size
+            out = lax.dynamic_update_slice_in_dim(out, held, owner * rows, axis=0)
+            if hop < size - 1:
+                held = lax.ppermute(held, "coarse", right)
+        coarse_full = out
         prolonged = jnp.dot(member_table, coarse_full, precision=highest)
         direction = local_part + prolonged[:, None] * basis_local
         directions.append(direction)

time: 971 us -> 938 us (0.966)
  matrix products: 73.9 us -> 13.6 us
  blocking collectives: 835 us -> 796 us
  waiting for transfers between devices: 0 us -> 25.1 us
  other arithmetic: 21.1 us -> 42.4 us
  starting transfers between devices: 0 us -> 10.6 us
    dot_general x4 -> x0, matrix products: 61.5 us -> none  [on_device(): jnp.einsum('bij,bj->bi', inverse_blocks, current + margin(current), preci...]
    all_gather x4 -> x0, blocking collectives: 38.7 us -> none  [on_device(): coarse_full = lax.all_gather(coarse_part, 'coarse', axis=0, tiled=True)]
    ppermute x0 -> x12, waiting for transfers between devices: none -> 25.1 us  [on_device(): held = lax.ppermute(held, 'coarse', right)]
    unnamed x0 -> x4, other arithmetic: none -> 22.5 us
    ppermute x0 -> x12, starting transfers between devices: none -> 10.6 us  [on_device(): held = lax.ppermute(held, 'coarse', right)]
  transfers between devices with their start and end apart: 0 -> 12, of which waited for: 0 -> 6; matrix products, arithmetic and copies ran while one was open for 0% -> 4% of each run, Pallas kernels for 0% -> 0%
where the time goes in v1:
time: 938 us; the launch traced here: 926 us
  blocking collectives  796 us (85%)
  other arithmetic  42.4 us (5%)
  waiting for transfers between devices  25.1 us (3%)
  between operations  21.1 us (2%)
  local copies, waits for them, and re-layouts  17.3 us (2%)
  matrix products  13.6 us (1%)
  starting transfers between devices  10.6 us (1%)
    all_gather x32, blocking collectives, margin(): gathered = lax.all_gather(outgoing[round_id], 'sub', axis=0, tiled=True)  279 us
    psum x5, blocking collectives, squared_norm(): return lax.psum(jnp.sum(values * values), ('sub', 'coarse'))  211 us
    psum x4, blocking collectives, on_device(): lax.psum(jnp.dot(inner, member_table, precision=highest) * factor, ('sub'...  158 us
    psum x4, blocking collectives, on_device(): lax.psum(jnp.stack([jnp.sum(vector * product) for vector in basis_list]),...  148 us
    ppermute x12, waiting for transfers between devices, on_device(): held = lax.ppermute(held, 'coarse', right)  25.1 us
    unnamed x4, other arithmetic  22.5 us
  transfers between devices with their start and end apart: 12, of which 6 were waited for; matrix products, arithmetic and copies ran while one was open for 4% of the time, Pallas kernels for 0%

profile of v1, /device:TPU:0, one launch (start us, length us, event | category | flops | bytes accessed | tf_op | source)
XLA Modules:
  0.0 926.2 jit_solution(8619355242627927982)
XLA Ops:
  0.0 1.5 multiply_reduce_fusion.14
  2.5 42.3 %psum.91 = f32[]{:T(128)} all-reduce(f32[]{:T(128)} %multiply_reduce_fusion.14), channel_id=1, replica_groups=mesh['sub'=8,'coarse'=4] {'sub','coarse'}, use_global_device_ids=true, to_apply=%region_1.0 | all-reduce | flops 1 | bytes 8 | tf_op jit(solution)/shard_map/psum | solution.py:94
  47.3 40.3 %psum.92 = f32[512]{0:T(512)S(1)} all-reduce(f32[512]{0:T(512)S(1)} %broadcast_multiply_fusion.3), channel_id=1, replica_groups=mesh['sub'=8,'coarse'=4] {'sub','coarse'}, use_global_device_ids=true, to_apply=%region_3.5 | all-reduce | flops 512 | bytes 4096 | tf_op jit(solution)/shard_map/psum | solution.py:104
  95.8 9.8 %all_gather.96 = f32[64,128]{1,0:T(8,128)S(1)} all-gather(f32[8,128]{1,0:T(8,128)S(1)} %get-tuple-element.63), channel_id=1, replica_groups=mesh['sub'=8,'coarse'=4] {'sub'}, dimensions={0}, use_global_device_ids=true | all-gather | bytes 36864 | tf_op jit(solution)/shard_map/all_gather | solution.py:82
  105.6 9.0 all_gather.99
  114.6 8.1 all_gather.98
  122.7 9.0 all_gather.97
  132.6 5.6 fusion
  139.8 3.9 collective-permute-done.1
  144.4 4.6 collective-permute-done.2
  150.3 8.1 all_gather.100
  158.4 9.0 all_gather.103
  167.4 8.1 all_gather.102
  175.5 9.0 all_gather.101
  186.3 37.1 %psum.93 = f32[]{:T(128)} all-reduce(f32[]{:T(128)} %get-tuple-element.80), channel_id=1, replica_groups=mesh['sub'=8,'coarse'=4] {'sub','coarse'}, use_global_device_ids=true, to_apply=%region_5.7 | all-reduce | flops 1 | bytes 8 | tf_op jit(solution)/shard_map/psum | solution.py:140
  224.7 42.3 %psum.94 = f32[]{:T(128)} all-reduce(f32[]{:T(128)} %multiply_reduce_fusion.12), channel_id=1, replica_groups=mesh['sub'=8,'coarse'=4] {'sub','coarse'}, use_global_device_ids=true, to_apply=%region_7.9 | all-reduce | flops 1 | bytes 8 | tf_op jit(solution)/shard_map/psum | solution.py:94
  268.7 39.6 %psum.95 = f32[512]{0:T(512)S(1)} all-reduce(f32[512]{0:T(512)S(1)} %broadcast_multiply_fusion.2), channel_id=1, replica_groups=mesh['sub'=8,'coarse'=4] {'sub','coarse'}, use_global_device_ids=true, to_apply=%region_9.11 | all-reduce | flops 512 | bytes 4096 | tf_op jit(solution)/shard_map/psum | solution.py:104
  308.5 2.2 collective-permute-start.3
  311.4 9.8 %all_gather.104 = f32[64,128]{1,0:T(8,128)S(1)} all-gather(f32[8,128]{1,0:T(8,128)S(1)} %get-tuple-element.55), channel_id=1, replica_groups=mesh['sub'=8,'coarse'=4] {'sub'}, dimensions={0}, use_global_device_ids=true | all-gather | bytes 36864 | tf_op jit(solution)/shard_map/all_gather | solution.py:82
  321.3 8.1 all_gather.107
  329.4 9.0 all_gather.106
  338.4 8.1 all_gather.105
  348.1 5.6 fusion.1
  356.7 3.8 collective-permute-done.5
  361.7 9.0 all_gather.108
  370.7 8.1 all_gather.111
  378.8 9.0 all_gather.110
  387.8 8.1 all_gather.109
  399.3 36.8 %psum.96 = f32[2]{0:T(128)S(1)} all-reduce(f32[2]{0:T(128)S(1)} %pad_maximum_fusion.8), channel_id=1, replica_groups=mesh['sub'=8,'coarse'=4] {'sub','coarse'}, use_global_device_ids=true, to_apply=%region_12.14 | all-reduce | flops 2 | bytes 16 | tf_op jit(solution)/shard_map/psum | solution.py:140
  436.8 1.9 multiply_reduce_fusion.9
  438.8 42.4 %psum.97 = f32[]{:T(128)} all-reduce(f32[]{:T(128)} %get-tuple-element.21), channel_id=1, replica_groups=mesh['sub'=8,'coarse'=4] {'sub','coarse'}, use_global_device_ids=true, to_apply=%region_14.16 | all-reduce | flops 1 | bytes 8 | tf_op jit(solution)/shard_map/psum | solution.py:94
  482.1 38.9 %psum.98 = f32[512]{0:T(512)S(1)} all-reduce(f32[512]{0:T(512)S(1)} %broadcast_multiply_fusion.1), channel_id=1, replica_groups=mesh['sub'=8,'coarse'=4] {'sub','coarse'}, use_global_device_ids=true, to_apply=%region_16.18 | all-reduce | flops 512 | bytes 4096 | tf_op jit(solution)/shard_map/psum | solution.py:104
  521.3 2.2 collective-permute-start.6
  524.2 9.8 %all_gather.112 = f32[64,128]{1,0:T(8,128)S(1)} all-gather(f32[8,128]{1,0:T(8,128)S(1)} %get-tuple-element.47), channel_id=1, replica_groups=mesh['sub'=8,'coarse'=4] {'sub'}, dimensions={0}, use_global_device_ids=true | all-gather | bytes 36864 | tf_op jit(solution)/shard_map/all_gather | solution.py:82
  534.0 9.0 all_gather.115
  543.0 8.1 all_gather.114
  551.1 9.0 all_gather.113
  561.7 5.6 fusion.2
  571.0 4.4 collective-permute-done.8
  576.7 8.1 all_gather.116
  584.9 9.0 all_gather.119
  593.8 8.1 all_gather.118
  602.0 9.0 all_gather.117
  612.9 2.0 pad_maximum_fusion.9
  614.9 36.8 %psum.99 = f32[3]{0:T(128)S(1)} all-reduce(f32[3]{0:T(128)S(1)} %pad_maximum_fusion.9), channel_id=1, replica_groups=mesh['sub'=8,'coarse'=4] {'sub','coarse'}, use_global_device_ids=true, to_apply=%region_20.22 | all-reduce | flops 3 | bytes 24 | tf_op jit(solution)/shard_map/psum | solution.py:140
  652.4 2.5 multiply_reduce_fusion.5
  654.9 41.6 %psum.100 = f32[]{:T(128)} all-reduce(f32[]{:T(128)} %get-tuple-element.17), channel_id=1, replica_groups=mesh['sub'=8,'coarse'=4] {'sub','coarse'}, use_global_device_ids=true, to_apply=%region_22.24 | all-reduce | flops 1 | bytes 8 | tf_op jit(solution)/shard_map/psum | solution.py:94
  697.5 39.6 %psum.101 = f32[512]{0:T(512)S(1)} all-reduce(f32[512]{0:T(512)S(1)} %broadcast_multiply_fusion), channel_id=1, replica_groups=mesh['sub'=8,'coarse'=4] {'sub','coarse'}, use_global_device_ids=true, to_apply=%region_24.26 | all-reduce | flops 512 | bytes 4096 | tf_op jit(solution)/shard_map/psum | solution.py:104
  737.3 2.2 collective-permute-start.9
  740.2 10.0 %all_gather.120 = f32[64,128]{1,0:T(8,128)S(1)} all-gather(f32[8,128]{1,0:T(8,128)S(1)} %get-tuple-element.39), channel_id=1, replica_groups=mesh['sub'=8,'coarse'=4] {'sub'}, dimensions={0}, use_global_device_ids=true | all-gather | bytes 36864 | tf_op jit(solution)/shard_map/all_gather | solution.py:82
  750.3 8.1 all_gather.123
  758.4 9.0 all_gather.122
  767.4 8.1 all_gather.121
  776.4 5.6 fusion.3
  786.7 3.9 collective-permute-done.10
  791.5 4.5 collective-permute-done.11
  797.2 9.0 all_gather.124
  806.2 8.1 all_gather.127
  814.3 9.0 all_gather.126
  823.3 8.1 all_gather.125
  833.4 2.6 pad_maximum_fusion.10
  836.0 36.8 %psum.102 = f32[4]{0:T(128)S(1)} all-reduce(f32[4]{0:T(128)S(1)} %pad_maximum_fusion.10), channel_id=1, replica_groups=mesh['sub'=8,'coarse'=4] {'sub','coarse'}, use_global_device_ids=true, to_apply=%region_29.31 | all-reduce | flops 4 | bytes 32 | tf_op jit(solution)/shard_map/psum | solution.py:140
  878.6 3.2 multiply_reduce_fusion
  881.8 42.5 %psum.103 = f32[]{:T(128)} all-reduce(f32[]{:T(128)} %multiply_reduce_fusion), channel_id=1, replica_groups=mesh['sub'=8,'coarse'=4] {'sub','coarse'}, use_global_device_ids=true, to_apply=%region_31.33 | all-reduce | flops 1 | bytes 8 | tf_op jit(solution)/shard_map/psum | solution.py:94
  (193 shorter events, 41.2 us)
Async XLA Ops:
  0.0 131.7 %copy-start = (f32[1,1,4,128,128]{4,3,2,1,0:T(8,128)S(1)}, f32[1,1,4,128,128]{4,3,2,1,0:T(8,128)}, u32[]{:S(2)}) copy-start(f32[1,1,4,128,128]{4,3,2,1,0:T(8,128)} %param.17) | copy-start | bytes 786436
  0.0 149.2 %copy-start.4 = (s32[1,1,128]{2,1,0:T(1,128)S(1)}, s32[1,1,128]{2,1,0:T(1,128)}, u32[]{:S(2)}) copy-start(s32[1,1,128]{2,1,0:T(1,128)} %param.23) | copy-start | bytes 1540
  0.0 308.3 %copy-start.1 = (f32[128,512]{1,0:T(8,128)S(1)}, f32[128,512]{1,0:T(8,128)}, u32[]{:S(2)}) copy-start(f32[128,512]{1,0:T(8,128)} %param.19) | copy-start | bytes 786436
  0.0 139.6 %copy-start.3 = (f32[1,1,128,128]{3,2,1,0:T(8,128)S(1)}, f32[1,1,128,128]{3,2,1,0:T(8,128)}, u32[]{:S(2)}) copy-start(f32[1,1,128,128]{3,2,1,0:T(8,128)} %param.14) | copy-start | bytes 196612
  0.0 139.7 %copy-start.2 = (f32[1,1,128,128]{3,2,1,0:T(8,128)S(1)}, f32[1,1,128,128]{3,2,1,0:T(8,128)}, u32[]{:S(2)}) copy-start(f32[1,1,128,128]{3,2,1,0:T(8,128)} %param.15) | copy-start | bytes 196612
  88.9 49.4 %collective-permute-start = (f32[128]{0:T(128)S(1)}, f32[128]{0:T(128)S(1)}, u32[]{:S(2)}, u32[]{:S(2)}) collective-permute-start(f32[128]{0:T(128)S(1)} %convolution_bitcast_fusion.7), channel_id=1, source_target_pairs={{0,1},{1,2},{2,3},{3,0},{4,5},{5,6},{6,7},{7,4},{8,9},{9,10},{10,1... | collective-permute-start | bytes 1544 | tf_op jit(solution)/shard_map/ppermute | solution.py:125
  138.3 5.4 collective-permute-start.1
  143.7 5.3 collective-permute-start.2
  308.5 38.9 %collective-permute-start.3 = (f32[128]{0:T(128)S(1)}, f32[128]{0:T(128)S(1)}, u32[]{:S(2)}, u32[]{:S(2)}) collective-permute-start(f32[128]{0:T(128)S(1)} %convolution_bitcast_fusion.5), channel_id=1, source_target_pairs={{0,1},{1,2},{2,3},{3,0},{4,5},{5,6},{6,7},{7,4},{8,9},{9,10},{10,1... | collective-permute-start | bytes 1544 | tf_op jit(solution)/shard_map/ppermute | solution.py:125
  347.4 7.6 collective-permute-start.4
  355.1 5.4 collective-permute-start.5
  521.3 39.7 %collective-permute-start.6 = (f32[128]{0:T(128)S(1)}, f32[128]{0:T(128)S(1)}, u32[]{:S(2)}, u32[]{:S(2)}) collective-permute-start(f32[128]{0:T(128)S(1)} %convolution_bitcast_fusion.3), channel_id=1, source_target_pairs={{0,1},{1,2},{2,3},{3,0},{4,5},{5,6},{6,7},{7,4},{8,9},{9,10},{10,1... | collective-permute-start | bytes 1544 | tf_op jit(solution)/shard_map/ppermute | solution.py:125
  561.0 9.1 collective-permute-start.7
  570.1 5.4 collective-permute-start.8
  737.3 47.9 %collective-permute-start.9 = (f32[128]{0:T(128)S(1)}, f32[128]{0:T(128)S(1)}, u32[]{:S(2)}, u32[]{:S(2)}) collective-permute-start(f32[128]{0:T(128)S(1)} %convolution_bitcast_fusion.1), channel_id=1, source_target_pairs={{0,1},{1,2},{2,3},{3,0},{4,5},{5,6},{6,7},{7,4},{8,9},{9,10},{10,1... | collective-permute-start | bytes 1544 | tf_op jit(solution)/shard_map/ppermute | solution.py:125
  785.2 5.4 collective-permute-start.10
  790.6 5.3 collective-permute-start.11
